TPU v7x, 32 devices: a whole 2x2x4 slice. The times are simulated.
32 devices in a mesh: seq: 8 (over z, core), head: 4 (over y, x).
Axes of the slice: x: 2, y: 2, z: 4, core: 2. Of those that a mesh axis runs over, the one named last changes fastest.
Arguments:
- qk_proj: bfloat16 [1024, 128], P('seq'), may hold values from -0.5 to 0.5
- values: bfloat16 [1024, 5120], P('seq', 'head'), may hold values from -0.59765625 to 0.59765625
- out_grad: bfloat16 [1024, 5120], P('seq', 'head'), may hold values from -1.5 to 1.5
- level_weights: float32 [80, 16, 1024], P('head', None, 'seq'), may hold values from 0.05 to 1
Outputs:
- qk_grad: float32 [1024, 128], P(('seq', 'head'))
- value_grad: bfloat16 [1024, 5120], P('seq', 'head')
- level_grad: float32 [80, 16, 1024], P('head', None, 'seq')
- carried_state: float32 [8, 128, 5120], P('seq', None, 'head')
All inputs are finite; a program needn't handle non-finite values.
Results may differ from a plain program's by a relative error of at most 0.0057.
Values sent between devices are 32-bit elements; how exact they have to be, the bound alone decides.
A program may use at most 64 MiB of HBM per device.

v0:
```python
import jax
import jax.numpy as jnp
from jax import lax
from jax.sharding import PartitionSpec as P


def from_partner(value, axis, distance):
    mask = 2**distance
    pairs = [(source, source ^ mask) for source in range(lax.axis_size(axis))]
    return lax.ppermute(value, axis, pairs)


def weight_matrix(weights_head, length, tok_bits):
    blocks = weights_head[0].reshape(length, 1, 1)
    for exponent in range(tok_bits):
        half_size = 1 << exponent
        block_count = length // (2 * half_size)
        paired = blocks.reshape(block_count, 2, half_size, half_size)
        top_half = paired[:, 0]
        bottom_half = paired[:, 1]
        row_weight = weights_head[exponent + 1].reshape(block_count, 2, half_size)[:, 1]
        fill_block = jnp.broadcast_to(row_weight[:, :, None], (block_count, half_size, half_size))
        upper_half = jnp.concatenate([top_half, jnp.zeros_like(top_half)], axis=2)
        lower_half = jnp.concatenate([fill_block, bottom_half], axis=2)
        blocks = jnp.concatenate([upper_half, lower_half], axis=1)
    return blocks.reshape(length, length)


def level_sums(product, length, tok_bits):
    current = product[None]
    found = []
    for exponent in range(tok_bits - 1, -1, -1):
        half_size = 1 << exponent
        block_count = current.shape[0]
        split = current.reshape(block_count, 2, half_size, 2, half_size)
        lower_sums = jnp.sum(split[:, 1, :, 0, :], axis=2)
        found.append(jnp.stack([jnp.zeros_like(lower_sums), lower_sums], axis=1).reshape(length))
        current = jnp.stack([split[:, 0, :, 0, :], split[:, 1, :, 1, :]], axis=1).reshape(
            2 * block_count, half_size, half_size
        )
    found.append(current.reshape(length))
    return jnp.stack(found[::-1], axis=0)


def body(qk_proj, values, out_grad, level_weights):
    tok_count = qk_proj.shape[0]
    inner_width = values.shape[1]
    head_count = level_weights.shape[0]
    level_count = level_weights.shape[1]
    head_dim = inner_width // head_count
    tok_bits = tok_count.bit_length() - 1
    seq_count = lax.axis_size("seq")
    seq_bits = seq_count.bit_length() - 1
    segment = lax.axis_index("seq")
    grad_float = out_grad.astype(jnp.float32)
    own_state = jnp.einsum("tn,tx->nx", qk_proj, values, preferred_element_type=jnp.float32)
    every_state = lax.all_gather(own_state[None], "seq", axis=0, tiled=True)
    others = jnp.arange(seq_count, dtype=jnp.int32)
    selectors = []
    for bit_pos in range(seq_bits):
        upper_part = jnp.right_shift(segment, bit_pos)
        chosen = (jnp.right_shift(others, bit_pos) == upper_part - 1) & (
            jnp.bitwise_and(upper_part, 1) == 1
        )
        selectors.append(chosen.astype(jnp.float32))
    level_state = jnp.einsum(
        "be,enx->bnx", jnp.stack(selectors), every_state, precision=lax.Precision.HIGHEST
    )
    carried = jnp.sum(level_state, axis=0)
    state_low = level_state.astype(jnp.bfloat16)
    cross_weights = level_weights[:, tok_bits + 1 : tok_bits + 1 + seq_bits, :]
    column_scale = jnp.repeat(jnp.transpose(cross_weights, (1, 2, 0)), head_dim, axis=2)
    scaled = (column_scale * grad_float[None]).astype(jnp.bfloat16)
    grad_state = jnp.einsum("tn,btx->bnx", qk_proj, scaled, preferred_element_type=jnp.float32)
    pending = grad_state
    back_state = jnp.zeros_like(own_state)
    for bit_pos in range(seq_bits):
        received = from_partner(pending, "seq", bit_pos)
        upper_bit = jnp.bitwise_and(jnp.right_shift(segment, bit_pos), 1)
        back_state = back_state + jnp.where(upper_bit == 0, received[0], 0.0)
        pending = pending[1:] + received[1:]
    back_low = back_state.astype(jnp.bfloat16)
    query_cross = jnp.einsum("btx,bnx->tn", scaled, state_low, preferred_element_type=jnp.float32)
    key_cross = jnp.einsum("tx,nx->tn", values, back_low, preferred_element_type=jnp.float32)
    value_cross = jnp.dot(qk_proj, back_low, preferred_element_type=jnp.float32)
    readout = jnp.einsum("tn,bnx->btx", qk_proj, state_low, preferred_element_type=jnp.float32)
    lam_cross = jnp.sum(
        (readout * grad_float[None]).reshape(seq_bits, tok_count, head_count, head_dim), axis=3
    )
    lam_cross = jnp.transpose(lam_cross, (2, 0, 1))
    score = jnp.einsum("tn,sn->ts", qk_proj, qk_proj, preferred_element_type=jnp.float32)
    vals_heads = jnp.transpose(values.reshape(tok_count, head_count, head_dim), (1, 0, 2))
    grads_heads = jnp.transpose(out_grad.reshape(tok_count, head_count, head_dim), (1, 0, 2))
    local_levels = level_weights[:, : tok_bits + 1, :]

    def one_head(head_ops):
        weights_head, grads_head, vals_head = head_ops
        pair_grad = jnp.einsum(
            "tp,sp->ts", grads_head, vals_head, preferred_element_type=jnp.float32
        )
        local_weight = weight_matrix(weights_head, tok_count, tok_bits)
        weighted_score = (local_weight * score).astype(jnp.bfloat16)
        weighted_grad = (local_weight * pair_grad).astype(jnp.bfloat16)
        value_head = jnp.einsum(
            "ts,tp->sp", weighted_score, grads_head, preferred_element_type=jnp.float32
        )
        qk_head = jnp.einsum(
            "ts,sn->tn", weighted_grad, qk_proj, preferred_element_type=jnp.float32
        )
        qk_head = qk_head + jnp.einsum(
            "ts,tn->sn", weighted_grad, qk_proj, preferred_element_type=jnp.float32
        )
        lam_head = level_sums(score * pair_grad, tok_count, tok_bits)
        return (value_head, qk_head, lam_head)

    value_heads, qk_heads, lam_local = lax.map(one_head, (local_levels, grads_heads, vals_heads))
    value_local = jnp.transpose(value_heads, (1, 0, 2)).reshape(tok_count, inner_width)
    query_local = jnp.sum(qk_heads, axis=0)
    unused_levels = level_count - tok_bits - 1 - seq_bits
    level_grad = jnp.concatenate(
        [lam_local, lam_cross, jnp.zeros((head_count, unused_levels, tok_count), jnp.float32)],
        axis=1,
    )
    value_grad = (value_local + value_cross).astype(jnp.bfloat16)
    qk_part = query_local + query_cross + key_cross
    qk_grad = lax.psum_scatter(qk_part, "head", scatter_dimension=0, tiled=True)
    return (qk_grad, value_grad, level_grad, carried[None])


def solution(mesh):
    in_specs = (P("seq", None), P("seq", "head"), P("seq", "head"), P("head", None, "seq"))
    out_specs = (
        P(("seq", "head"), None),
        P("seq", "head"),
        P("head", None, "seq"),
        P("seq", None, "head"),
    )
    return jax.shard_map(body, mesh=mesh, in_specs=in_specs, out_specs=out_specs, check_vma=False)
```

profile of v0, /device:TPU:0, one launch (start us, length us, event | category | flops | bytes accessed | tf_op | source)
XLA Modules:
  0.0 364.8 jit_solution(13299229745283530131)
XLA Ops:
  8.1 1.1 copy.232
  10.4 3.6 collective-permute-done
  14.2 1.2 copy-done.4
  15.3 2.9 collective-permute-start.1
  18.3 1.1 fusion.44
  19.5 1.9 copy.227
  22.4 63.6 %collective-permute-done.1 = f32[2,128,1280]{1,2,0:T(8,128)} collective-permute-done((f32[2,128,1280]{1,2,0:T(8,128)S(1)}, f32[2,128,1280]{1,2,0:T(8,128)}, u32[]{:S(2)}, u32[]{:S(2)}) %collective-permute-start.1) | collective-permute-done | bytes 1310752 | tf_op jit(solution)/shard_map/ppermute | solution.py:10
  86.0 2.0 slice_add_fusion.1
  88.0 3.4 collective-permute-start.2
  91.5 221.5 %while.14 = (s32[]{:T(128)}, f32[20,128,64]{1,2,0:T(8,128)}, f32[20,128,128]{2,1,0:T(8,128)}, f32[20,8,128]{2,1,0:T(8,128)S(1)}, f32[20,8,128]{2,1,0:T(8,128)S(1...) while((s32[]{:T(128)}, f32[20,128,64]{1,2,0:T(8,128)}, ...), condition=%wide.region_7.8_spmd, body=%wide.region_0.7_spmd.sunk | while | flops 12818818 | bytes 2038941 | solution.py:116
  94.4 0.9 fusion.84
  100.3 1.5 fusion.83
  105.5 0.9 fusion.84
  111.3 1.5 fusion.83
  116.5 0.9 fusion.84
  122.4 1.5 fusion.83
  127.6 0.9 fusion.84
  133.5 1.5 fusion.83
  138.7 0.9 fusion.84
  144.6 1.5 fusion.83
  155.6 1.5 fusion.83
  160.8 0.9 fusion.84
  166.7 1.5 fusion.83
  171.9 0.9 fusion.84
  177.8 1.5 fusion.83
  188.9 1.5 fusion.83
  200.0 1.5 fusion.83
  211.0 1.5 fusion.83
  216.2 0.9 fusion.84
  222.1 1.5 fusion.83
  227.3 0.9 fusion.84
  233.2 1.5 fusion.83
  244.3 1.5 fusion.83
  255.3 1.5 fusion.83
  260.5 0.9 fusion.84
  266.4 1.5 fusion.83
  271.6 0.9 fusion.84
  277.5 1.5 fusion.83
  288.6 1.5 fusion.83
  293.7 0.9 fusion.84
  299.6 1.5 fusion.83
  310.7 1.5 fusion.83
  313.0 1.4 reduce_sum.85
  314.5 1.5 fusion.30
  317.9 10.2 %fusion.41 = (f32[128,1280]{1,0:T(8,128)}, bf16[3,128,1280]{2,0,1:T(4,128)(2,1)S(1)}) fusion(f32[8,128,1280]{2,1,0:T(8,128)} %bitcast.304, pred[1,8]{1,0:T(4,128)(4,1)S(1)} %get-tuple-element.192, pred[1,8]{1,0:T(4,128)(4,1)S(1)} %get-tuple-element.193, pred[1,8]{1,0:T(4,128)(4,1)S(1)} %compare_and_fusion.2), kind=kOutput, calls=%fused_computation.116 | convolution fusion | flops 48005168 | bytes 6881304 | tf_op jit(solution)/shard_map/be,enx->bnx/dot_general | solution.py:66
  328.1 1.7 fusion.21
  329.8 1.8 reduce_sum.86
  334.2 23.8 %reduce-scatter.2.cloned.1.call-done = f32[32,128]{1,0:T(8,128)} async-done(((f32[128,128]{1,0:T(8,128)}), f32[32,128]{1,0:T(8,128)}) %reduce-scatter.2.cloned.1.call-update) | async-done | bytes 16400 | tf_op jit(solution)/shard_map/reduce_scatter | solution.py:126
  (1968 shorter events, 181.6 us)
Async XLA Ops:
  7.2 310.7 %all-gather.3.cloned.1.call-start = ((), (), s32[]{:S(2)}) async-start(), calls=%async_computation.2 | async-start | bytes 5898240 | tf_op jit(solution)/shard_map/all_gather | solution.py:57
  8.1 1.3 copy-start
  9.8 8.4 %copy-start.1 = (bf16[128,1280]{1,0:T(8,128)(2,1)S(1)}, bf16[128,1280]{1,0:T(8,128)(2,1)}, u32[]{:S(2)}) copy-start(bf16[128,1280]{1,0:T(8,128)(2,1)} %param.7) | copy-start | bytes 983044
  9.9 4.2 %collective-permute-start = (f32[3,128,1280]{1,2,0:T(8,128)S(1)}, f32[3,128,1280]{1,2,0:T(8,128)S(1)}, u32[]{:S(2)}, u32[]{:S(2)}) collective-permute-start(f32[3,128,1280]{1,2,0:T(8,128)S(1)} %convolution_bitcast_fusion.2), channel_id=1, source_target_pairs={{0,4},{4,0},{8,12},{12,8},{16,20},{20,16},{24,28},{28,24},{1,5},{5... | collective-permute-start | bytes 5898248 | tf_op jit(solution)/shard_map/ppermute | solution.py:10
  14.0 1.3 copy-start.4
  15.3 70.7 %collective-permute-start.1 = (f32[2,128,1280]{1,2,0:T(8,128)S(1)}, f32[2,128,1280]{1,2,0:T(8,128)}, u32[]{:S(2)}, u32[]{:S(2)}) collective-permute-start(f32[2,128,1280]{1,2,0:T(8,128)S(1)} %slice_add_fusion), channel_id=1, source_target_pairs={{0,8},{4,12},{8,0},{12,4},{16,24},{20,28},{24,16},{28,20},{1,9},{5... | collective-permute-start | bytes 3932168 | tf_op jit(solution)/shard_map/ppermute | solution.py:10
  19.4 338.6 %reduce-scatter.2.cloned.1.call-start = ((), (), s32[]{:S(2)}) async-start(), calls=%async_computation.1 | async-start | bytes 81920 | tf_op jit(solution)/shard_map/reduce_scatter | solution.py:126
  21.3 70.1 %slice-start = ((f32[20,16,128]{2,1,0:T(8,128)}), f32[20,8,128]{2,1,0:T(8,128)S(1)}, s32[]{:S(2)}) async-start(f32[20,16,128]{2,1,0:T(8,128)} %param.9), calls=%async_computation.3 | async-start | bytes 163840 | tf_op jit(solution)/shard_map/slice | solution.py:94
  88.0 226.5 %collective-permute-start.2 = (f32[1,128,1280]{1,2,0:T(8,128)}, f32[1,128,1280]{1,2,0:T(8,128)S(1)}, u32[]{:S(2)}, u32[]{:S(2)}) collective-permute-start(f32[1,128,1280]{1,2,0:T(8,128)} %slice_add_fusion.1), channel_id=1, source_target_pairs={{0,16},{4,20},{8,24},{12,28},{16,0},{20,4},{24,8},{28,12},{1,17},{... | collective-permute-start | bytes 1966088 | tf_op jit(solution)/shard_map/ppermute | solution.py:10
  314.4 2.3 copy-start.5
  316.0 0.7 copy-start.2
  331.6 1.0 copy-start.3
Sparse Core Ops, SparseCore 0:
  19.5 71.5 all-gather.2
  333.6 24.3 reduce-scatter.1
where the time goes:
time: 371 us; the launch traced here: 365 us
  local copies, waits for them, and re-layouts  117 us (32%)
  waiting for transfers between devices  91 us (25%)
  matrix products  81.9 us (22%)
  other arithmetic  46.5 us (13%)
  between operations  14.2 us (4%)
  starting transfers between devices  7 us (2%)
  loops' own time  7 us (2%)
    ppermute x3, waiting for transfers between devices, from_partner(): return lax.ppermute(value, axis, pairs)  67.2 us
    dot_general x20, matrix products, one_head(): jnp.einsum('ts,tp->sp', weighted_score, grads_head, preferred_element_typ...  29.6 us
    reduce_sum x120, other arithmetic, level_sums(): lower_sums = jnp.sum(split[:, 1, :, 0, :], axis=2)  29.2 us
    reduce_scatter x1, waiting for transfers between devices, body(): qk_grad = lax.psum_scatter(qk_part, 'head', scatter_dimension=0, tiled=True)  23.8 us
    another operation x180, local copies, waits for them, and re-layouts, level_sums(): jnp.stack([split[:, 0, :, 0, :], split[:, 1, :, 1, :]], axis=1)  19 us
    dot_general x20, matrix products, one_head(): jnp.einsum('tp,sp->ts', grads_head, vals_head, preferred_element_type=jnp...  18.5 us
    reshape x160, local copies, waits for them, and re-layouts, level_sums(): return jnp.stack(found[::-1], axis=0)  17.5 us
    dot_general x20, matrix products, one_head(): jnp.einsum('ts,tn->sn', weighted_grad, qk_proj, preferred_element_type=jn...  16 us
  transfers between devices with their start and end apart: 5, of which 3 were waited for; matrix products, arithmetic and copies ran while one was open for 62% of the time, Pallas kernels for 0%

commit v1 on v0

v1 whole, which is shorter than its diff:
```python
import functools

import jax
import jax.numpy as jnp
from jax import lax
from jax.experimental import pallas as pl
from jax.experimental.pallas import tpu as pltpu
from jax.sharding import PartitionSpec as P

MESH = pl.DeviceIdType.MESH
CHUNKS = 4
F32 = jnp.float32
BF16 = jnp.bfloat16


def dot(a, b, ca, cb):
    return lax.dot_general(a, b, (((ca,), (cb,)), ((), ())), preferred_element_type=F32)


class Ids:
    def __init__(self):
        self.table = {}

    def __call__(self, *key):
        return self.table.setdefault(key, len(self.table))


def sem_ids(chips, heads, chip_bits):
    send, recv = Ids(), Ids()
    for r in range(CHUNKS):
        for ids in (send, recv):
            ids("xa", r), ids("xb", r), ids("rd", r)
            for k in range(chip_bits):
                ids("xd", k, r), ids("ru", k, r)
                ids("up", k, r), ids("dn", k, r)
        for k in range(chip_bits):
            send("dc", k, r)
            for i in range(1 << k):
                send("up", k, r, i), send("dn", k, r, i)
                recv("dc", k, r, i)
    send("xc"), recv("xc")
    for i in range(heads):
        send("rs", i), recv("rs", i)
    return send, recv


def kernel(chips, head_parts, seq_bits, qk_ref, v_ref, g_ref, lw_ref, qg_ref, vg_ref, lam_ref, car_ref,
           own, gst, xup, xd0, xd, bz, gz, acc, dsum, lst, dcon, drec, bh, bo, bst, low, blow, sc, vloc, at, qp, rs,
           lev_ref, ssem, rsem):
    tok, state = qk_ref.shape
    width = v_ref.shape[1]
    nheads, levels = lw_ref.shape[0], lw_ref.shape[1]
    hdim = width // nheads
    tok_bits = tok.bit_length() - 1
    chip_bits = seq_bits - 1
    half = state // 2
    rows = half // CHUNKS
    sid, rid = sem_ids(chips, head_parts, chip_bits)

    seq, hd = lax.axis_index("seq"), lax.axis_index("head")
    core, z = seq % 2, seq // 2
    partner = seq + 1 - 2 * core

    def bit(k):
        return (z // (1 << k)) % 2

    def at_chip(chip):
        return {"seq": chip * 2 + core}

    mines = [pl.ds(pl.multiple_of(core * half + r * rows, rows), rows) for r in range(CHUNKS)]
    others = [pl.ds(pl.multiple_of((1 - core) * half + r * rows, rows), rows) for r in range(CHUNKS)]
    mine, other = mines.__getitem__, others.__getitem__

    def part(r):
        return pl.ds(r * rows, rows)

    started = []

    def send(cond, src, dst, skey, rkey, device):
        pltpu.make_async_remote_copy(
            src_ref=src, dst_ref=dst, send_sem=ssem.at[sid(*skey)], recv_sem=rsem.at[rid(*rkey)],
            device_id=device, device_id_type=MESH).start()
        started.append((cond, skey))

    def sent(skey):
        like = xd0 if skey[0] == "xc" else rs.at[skey[1]] if skey[0] == "rs" else bz.at[part(0)]
        pltpu.make_async_remote_copy(
            src_ref=like, dst_ref=like, send_sem=ssem.at[sid(*skey)], recv_sem=rsem.at[0],
            device_id={"seq": partner}, device_id_type=MESH).wait_send()

    def arrive(ref, rkey):
        pltpu.make_async_remote_copy(
            src_ref=ref, dst_ref=ref, send_sem=ssem.at[0], recv_sem=rsem.at[rid(*rkey)],
            device_id={"seq": partner}, device_id_type=MESH).wait_recv()

    barrier = pltpu.get_barrier_semaphore()
    pl.semaphore_signal(barrier, inc=1, device_id={"seq": partner}, device_id_type=MESH)
    for i in range(1, chips):
        pl.semaphore_signal(barrier, inc=1, device_id=at_chip((z + i) % chips), device_id_type=MESH)
    for i in range(1, head_parts):
        pl.semaphore_signal(barrier, inc=1, device_id={"head": (hd + i) % head_parts}, device_id_type=MESH)

    qk = qk_ref[...]
    own[...] = dot(qk, v_ref[...], 0, 0)
    pl.semaphore_wait(barrier, 1 + (chips - 1) + (head_parts - 1))
    for r in range(CHUNKS):
        send(None, own.at[other(r)], xup.at[other(r)], ("xa", r), ("xa", r), {"seq": partner})

    spread = (lax.broadcasted_iota(jnp.int32, (nheads, width), 1) // hdim
              == lax.broadcasted_iota(jnp.int32, (nheads, width), 0)).astype(F32).astype(BF16)

    def grad_state(b):
        weight = lw_ref[:, tok_bits + 1 + b, :]
        first = weight.astype(BF16)
        rest = weight - first.astype(F32)
        second = rest.astype(BF16)
        third = (rest - second.astype(F32)).astype(BF16)
        scale = dot(first, spread, 0, 0) + (dot(second, spread, 0, 0) + dot(third, spread, 0, 0))
        scaled = (scale * g_ref[...].astype(F32)).astype(BF16)
        sc[b] = scaled
        gst[b] = dot(qk, scaled, 0, 0)

    for k in range(chip_bits - 1, -1, -1):
        grad_state(k + 1)
        for r in range(CHUNKS):
            send(None, gst.at[k + 1, other(r)], xd.at[k, part(r)], ("xd", k, r), ("xd", k, r), {"seq": partner})

    for r in range(CHUNKS):
        arrive(xup.at[mine(r)], ("xa", r))
        bz[part(r)] = own[mine(r)] + xup[mine(r)]
        if chip_bits:
            cond = bit(0) == 0

            @pl.when(cond)
            def _():
                send(cond, bz.at[part(r)], lst.at[0, mine(r)], ("up", 0, r, 0), ("up", 0, r), at_chip(z + 1))

        for k in range(chip_bits - 1, -1, -1):
            arrive(xd.at[k, part(r)], ("xd", k, r))
            gz[k, part(r)] = gst[k + 1, mine(r)] + xd[k, part(r)]
            size = 1 << k
            under = z % size
            if k == 0:
                cond_d = bit(0) == 1

                @pl.when(cond_d)
                def _():
                    send(cond_d, gz.at[0, part(r)], drec.at[0, part(r)], ("dn", 0, r, 0), ("dn", 0, r), at_chip(z - 1))
            for i in range(1, size):
                cond_c = (bit(k) == 1) & (under == i)

                @pl.when(cond_c)
                def _():
                    send(cond_c, gz.at[k, part(r)], dcon.at[size - 1 - k + i - 1, part(r)],
                         ("dc", k, r), ("dc", k, r, i), at_chip(z - i))

    cond_low = core == 0
    cond_high = core == 1

    @pl.when(cond_low)
    def _():
        for r in range(CHUNKS):
            send(cond_low, own.at[mine(r)], xup.at[mine(r)], ("xb", r), ("xb", r), {"seq": partner})

    grad_state(0)

    @pl.when(cond_high)
    def _():
        send(cond_high, gst.at[0], xd0, ("xc",), ("xc",), {"seq": partner})

    key_at = lax.broadcasted_iota(jnp.int32, (tok, tok), 0)
    query_at = lax.broadcasted_iota(jnp.int32, (tok, tok), 1)
    crossed = key_at ^ query_at
    found = jnp.zeros((tok, tok), jnp.int32)
    for exponent in range(tok_bits):
        found = found + jnp.where(crossed >= (1 << exponent), 1, 0)
    lev_ref[0] = jnp.where(key_at <= query_at, found, -1).astype(F32)
    lev_ref[1] = dot(qk, qk, 1, 1)
    at[...] = jnp.zeros_like(at)
    lam_ref[:, tok_bits + 1 + seq_bits:, :] = jnp.zeros((nheads, levels - tok_bits - 1 - seq_bits, tok), F32)

    def head_group(head, cols, count):
        vals, grads = v_ref[:, cols], g_ref[:, cols]
        lane_head = lax.broadcasted_iota(jnp.int32, vals.shape, 1) // hdim
        score_parts, grad_parts = [], []
        total = at[...]
        for j in range(count):
            vals_j = vals if count == 1 else jnp.where(lane_head == j, vals, jnp.zeros_like(vals))
            grads_j = grads if count == 1 else jnp.where(lane_head == j, grads, jnp.zeros_like(grads))
            pair = dot(vals_j, grads, 1, 1)
            lev, score = lev_ref[0], lev_ref[1]
            weights = lw_ref[head + j]
            product = score * pair
            local = jnp.zeros((tok, tok), F32)
            sums = []
            for level in range(tok_bits + 1):
                here = lev == float(level)
                local = jnp.where(here, weights[level:level + 1, :], local)
                sums.append(jnp.sum(jnp.where(here, product, 0.0), axis=0, keepdims=True))
            lam_ref[head + j, 0:tok_bits + 1, :] = jnp.concatenate(sums, axis=0)
            score_parts.append((local * score).astype(BF16))
            grad_parts.append(grads_j)
            total = total + (local * pair).astype(BF16).astype(F32)
        at[...] = total
        out = dot(score_parts[0], grad_parts[0], 1, 0)
        for j in range(1, count):
            out = out + dot(score_parts[j], grad_parts[j], 1, 0)
        vloc[:, cols] = out

    per = max(1, 128 // hdim)
    groups = nheads // per

    def run_groups(start, stop):
        @pl.loop(start, stop)
        def _(p):
            head_group(p * per, pl.ds(pl.multiple_of(p * per * hdim, per * hdim), per * hdim), per)

    def up_step(k, r):
        cond = bit(k) == 1

        @pl.when(cond)
        def _():
            arrive(lst.at[k, mine(r)], ("up", k, r))
            send(cond, lst.at[k, mine(r)], lst.at[k, mine(r)], ("ru", k, r), ("ru", k, r), {"seq": partner})

        kk = k + 1
        if kk < chip_bits:
            size = 1 << kk
            cond_s = (z % size == size - 1) & (bit(kk) == 0)

            @pl.when(cond_s)
            def _():
                value = bz[part(r)]
                for j in range(kk):
                    value = value + lst[j, mine(r)]
                acc[kk, part(r)] = value
                for i in range(size - 1, -1, -1):
                    send(cond_s, acc.at[kk, part(r)], lst.at[kk, mine(r)], ("up", kk, r, i), ("up", kk, r),
                         at_chip(z + 1 + i))

            cond_d = (z % size == 0) & (bit(kk) == 1)

            @pl.when(cond_d)
            def _():
                value = gz[kk, part(r)]
                for i in range(1, size):
                    slot = size - 1 - kk + i - 1
                    arrive(dcon.at[slot, part(r)], ("dc", kk, r, i))
                    value = value + dcon[slot, part(r)]
                dsum[kk, part(r)] = value
                for i in range(size):
                    send(cond_d, dsum.at[kk, part(r)], drec.at[kk, part(r)], ("dn", kk, r, i), ("dn", kk, r),
                         at_chip(z - size + i))

    has_back = z != chips - 1

    def down_step(r):
        bh[part(r)] = jnp.zeros((rows, width), F32)
        for k in range(chip_bits):
            @pl.when(bit(k) == 0)
            def _():
                arrive(drec.at[k, part(r)], ("dn", k, r))
                bh[part(r)] = bh[part(r)] + drec[k, part(r)]

        @pl.when(has_back)
        def _():
            send(has_back, bh.at[part(r)], bo.at[part(r)], ("rd", r), ("rd", r), {"seq": partner})

    def cross(b):
        state_low = low[b]
        readout = dot(qk, state_low, 1, 0)
        product = readout * g_ref[...].astype(F32)
        high = product.astype(BF16)
        rest = (product - high.astype(F32)).astype(BF16)
        lam_ref[:, tok_bits + 1 + b, :] = dot(spread, high, 1, 1) + dot(spread, rest, 1, 1)
        part_b = dot(sc[b], state_low, 1, 1)
        if b == 0:
            qp[...] = part_b
        else:
            qp[...] = qp[...] + part_b

    def level_zero():
        @pl.when(core == 1)
        def _():
            for r in range(CHUNKS):
                arrive(xup.at[other(r)], ("xb", r))
            low[0] = xup[...].astype(BF16)
            car_ref[0] = xup[...]

        @pl.when(core == 0)
        def _():
            low[0] = jnp.zeros((state, width), BF16)
            car_ref[0] = jnp.zeros((state, width), F32)

        cross(0)

    def level_up(k):
        cond = bit(k) == 1

        @pl.when(cond)
        def _():
            for r in range(CHUNKS):
                arrive(lst.at[k, other(r)], ("ru", k, r))
            low[k + 1] = lst[k].astype(BF16)
            car_ref[0] = car_ref[0] + lst[k]

        @pl.when(jnp.logical_not(cond))
        def _():
            low[k + 1] = jnp.zeros((state, width), BF16)

        cross(k + 1)

    steps = [(lambda r=r: up_step(0, r)) for r in range(CHUNKS)] if chip_bits else []
    steps.append(level_zero)
    for k in range(1, chip_bits):
        if k == chip_bits - 1:
            for r in range(CHUNKS):
                steps.append(lambda r=r, k=k: (up_step(k, r), down_step(r)))
        else:
            steps += [(lambda r=r, k=k: up_step(k, r)) for r in range(CHUNKS)]
    if chip_bits < 2:
        steps += [(lambda r=r: down_step(r)) for r in range(CHUNKS)]
    slots = min(5, max(1, groups))
    done = 0
    for n, step in enumerate(steps):
        upto = groups * min(slots, n * slots // len(steps) + 1) // slots
        if upto > done:
            run_groups(done, upto)
            done = upto
        step()
    if done < groups:
        run_groups(done, groups)
    for h in range(groups * per, nheads):
        head_group(h, pl.ds(h * hdim, hdim), 1)

    high = at[...].astype(BF16)
    rest = (at[...] - high.astype(F32)).astype(BF16)
    qp[...] = qp[...] + (dot(high, qk, 1, 0) + dot(high, qk, 0, 0)) + (dot(rest, qk, 1, 0) + dot(rest, qk, 0, 0))

    for k in range(chip_bits):
        level_up(k)

    @pl.when(has_back)
    def _():
        for r in range(CHUNKS):
            arrive(bo.at[part(r)], ("rd", r))
            bst[mine(r)] = bh[part(r)]
            bst[other(r)] = bo[part(r)]

    @pl.when(jnp.logical_not(has_back))
    def _():
        bst[...] = jnp.zeros((state, width), F32)

    @pl.when(core == 0)
    def _():
        arrive(xd0, ("xc",))
        blow[...] = (bst[...] + xd0[...]).astype(BF16)

    @pl.when(core == 1)
    def _():
        blow[...] = bst[...].astype(BF16)

    back = blow[...]
    qp[...] = qp[...] + dot(v_ref[...], back, 1, 1)
    share = tok // head_parts
    for i in range(1, head_parts):
        to = (hd + i) % head_parts
        send(None, qp.at[pl.ds(pl.multiple_of(to * share, share), share)], rs.at[i], ("rs", i), ("rs", i), {"head": to})
    vg_ref[...] = (vloc[...] + dot(qk, back, 1, 0)).astype(BF16)
    total = qp[pl.ds(pl.multiple_of(hd * share, share), share)]
    for i in range(1, head_parts):
        arrive(rs.at[i], ("rs", i))
        total = total + rs[i]
    qg_ref[...] = total

    for cond, skey in started:
        if cond is None:
            sent(skey)
        else:
            @pl.when(cond)
            def _():
                sent(skey)


def solution(mesh):
    chips = mesh.shape["seq"] // 2
    head_parts = mesh.shape["head"]
    seq_bits = mesh.shape["seq"].bit_length() - 1
    chip_bits = seq_bits - 1

    def body(qk_proj, values, out_grad, level_weights):
        tok, state = qk_proj.shape
        width = values.shape[1]
        nheads, levels = level_weights.shape[:2]
        half = state // 2
        send, recv = sem_ids(chips, head_parts, chip_bits)
        bits = max(1, chip_bits)
        slots = max(1, (1 << chip_bits) - 1 - chip_bits)
        vm = pltpu.VMEM
        vspec = pl.BlockSpec(memory_space=pltpu.VMEM)
        return pl.pallas_call(
            functools.partial(kernel, chips, head_parts, seq_bits),
            out_shape=(
                jax.ShapeDtypeStruct((tok // head_parts, state), F32),
                jax.ShapeDtypeStruct((tok, width), BF16),
                jax.ShapeDtypeStruct((nheads, levels, tok), F32),
                jax.ShapeDtypeStruct((1, state, width), F32),
            ),
            in_specs=[vspec] * 4,
            out_specs=(vspec,) * 4,
            scratch_shapes=[
                vm((state, width), F32),
                vm((seq_bits, state, width), F32),
                vm((state, width), F32),
                vm((state, width), F32),
                vm((bits, half, width), F32),
                vm((half, width), F32),
                vm((bits, half, width), F32),
                vm((bits, half, width), F32),
                vm((bits, half, width), F32),
                vm((bits, state, width), F32),
                vm((slots, half, width), F32),
                vm((bits, half, width), F32),
                vm((half, width), F32),
                vm((half, width), F32),
                vm((state, width), F32),
                vm((seq_bits, state, width), BF16),
                vm((state, width), BF16),
                vm((seq_bits, tok, width), BF16),
                vm((tok, width), F32),
                vm((tok, tok), F32),
                vm((tok, state), F32),
                vm((head_parts, tok // head_parts, state), F32),
                vm((2, tok, tok), F32),
                pltpu.SemaphoreType.DMA((len(send.table),)),
                pltpu.SemaphoreType.DMA((len(recv.table),)),
            ],
            compiler_params=pltpu.CompilerParams(
                collective_id=0, has_side_effects=True, vmem_limit_bytes=56 * 1024 * 1024),
        )(qk_proj, values, out_grad, level_weights)

    return jax.shard_map(
        body, mesh=mesh,
        in_specs=(P("seq", None), P("seq", "head"), P("seq", "head"), P("head", None, "seq")),
        out_specs=(P(("seq", "head"), None), P("seq", "head"), P("head", None, "seq"), P("seq", None, "head")),
        check_vma=False)
```

time: 371 us -> 41 us (0.11); the launches traced: 365 us -> 40.8 us
  local copies, waits for them, and re-layouts: 117 us -> 5.54 us
  waiting for transfers between devices: 91 us -> 0 us
  matrix products: 81.9 us -> 0 us
  other arithmetic: 46.5 us -> 0 us
  Pallas kernels: 0 us -> 34.6 us
  between operations: 14.2 us -> 0.65 us
  loops' own time: 7 us -> 0 us
  starting transfers between devices: 7 us -> 0 us
    dot_general x88 -> x0, matrix products: 81.9 us -> none  [the longest x20 29.6 us: one_head(): jnp.einsum('ts,tp->sp', weighted_score, grads_head, preferred_element_typ...]
    ppermute x3 -> x0, waiting for transfers between devices: 67.2 us -> none  [from_partner(): return lax.ppermute(value, axis, pairs)]
    pallas_call x0 -> x1, Pallas kernels: none -> 34.6 us  [body(): pl.pallas_call(functools.partial(kernel, chips, head_parts, seq_bits), ou...]
    reduce_sum x122 -> x0, other arithmetic: 32.3 us -> none  [the longest x120 29.2 us: level_sums(): lower_sums = jnp.sum(split[:, 1, :, 0, :], axis=2)]
    reshape x280 -> x0, local copies, waits for them, and re-layouts: 32.1 us -> none  [the longest x160 17.5 us: level_sums(): return jnp.stack(found[::-1], axis=0)]
    reduce_scatter x1 -> x0, waiting for transfers between devices: 23.8 us -> none  [body(): qk_grad = lax.psum_scatter(qk_part, 'head', scatter_dimension=0, tiled=True)]
    another operation x340 -> x0, local copies, waits for them, and re-layouts: 22.8 us -> none  [the longest x180 19 us: level_sums(): jnp.stack([split[:, 0, :, 0, :], split[:, 1, :, 1, :]], axis=1)]
    squeeze x260 -> x0, local copies, waits for them, and re-layouts: 18.6 us -> none  [the longest x140 15 us: weight_matrix(): weights_head[exponent + 1].reshape(block_count, 2, half_size)[:, 1]]
  transfers between devices with their start and end apart: 5 -> 0, of which waited for: 3 -> 0; matrix products, arithmetic and copies ran while one was open for 62% -> 0% of each run, Pallas kernels for 0% -> 0%
where the time goes in v1:
time: 41 us; the launch traced here: 40.8 us
  Pallas kernels  34.6 us (84%)
  local copies, waits for them, and re-layouts  5.54 us (14%)
  between operations  0.65 us (2%)
    pallas_call x1, Pallas kernels, body(): pl.pallas_call(functools.partial(kernel, chips, head_parts, seq_bits), ou...  34.6 us
    unnamed x6, local copies, waits for them, and re-layouts  5.54 us

profile of v1, /device:TPU:0, one launch (start us, length us, event | category | flops | bytes accessed | tf_op | source)
XLA Modules:
  0.0 40.8 jit_solution(11065805038222665155)
XLA Ops:
  0.6 34.6 %shard_map.75 = (f32[32,128]{1,0:T(8,128)}, bf16[128,1280]{1,0:T(8,128)(2,1)}, f32[20,16,128]{2,1,0:T(8,128)}, f32[1,128,1280]{2,1,0:T(8,128)}) custom-call(bf16[128,128]{1,0:T(8,128)(2,1)} %qk_ref.1, bf16[128,1280]{1,0:T(8,128)(2,1)} %v_ref.1, bf16[128,1280]{1,0:T(8,128)(2,1)} %g_ref.1, f32[20,16,128]{2,1,0:T(8,128)} %lw_ref.1), custom_call_target="tpu_custom_call" | custom-call | tf_op jit(solution)/shard_map/pallas_call | solution.py:401
  35.2 0.0 copy-start
  35.3 1.4 %copy.12 = f32[32,128]{1,0:T(8,128)} copy(f32[32,128]{1,0:T(8,128)} %get-tuple-element.8) | data formatting | bytes 32768
  36.6 1.7 %copy.13 = bf16[128,1280]{1,0:T(8,128)(2,1)} copy(bf16[128,1280]{1,0:T(8,128)(2,1)} %get-tuple-element.9) | data formatting | bytes 655360
  38.4 1.6 %copy.14 = f32[20,16,128]{2,1,0:T(8,128)} copy(f32[20,16,128]{2,1,0:T(8,128)} %get-tuple-element.10) | data formatting | bytes 327680
  40.0 0.0 copy-done
  40.0 0.8 %copy.15 = f32[1,128,1280]{2,1,0:T(8,128)} copy(f32[1,128,1280]{2,1,0:T(8,128)S(1)} %copy-done) | data formatting | bytes 1310720
Async XLA Ops:
  35.2 4.7 %copy-start = (f32[1,128,1280]{2,1,0:T(8,128)S(1)}, f32[1,128,1280]{2,1,0:T(8,128)}, u32[]{:S(2)}) copy-start(f32[1,128,1280]{2,1,0:T(8,128)} %get-tuple-element.11) | copy-start | bytes 1966084

commit v2 on v1

--- a/solution.py
+++ b/solution.py
@@ -8,7 +8,7 @@
 from jax.sharding import PartitionSpec as P
 
 MESH = pl.DeviceIdType.MESH
-CHUNKS = 4
+CHUNKS = 8
 F32 = jnp.float32
 BF16 = jnp.bfloat16
 
@@ -25,23 +25,16 @@
         return self.table.setdefault(key, len(self.table))
 
 
-def sem_ids(chips, heads, chip_bits):
-    send, recv = Ids(), Ids()
+def sem_ids(heads, chip_bits):
+    ids = Ids()
     for r in range(CHUNKS):
-        for ids in (send, recv):
-            ids("xa", r), ids("xb", r), ids("rd", r)
-            for k in range(chip_bits):
-                ids("xd", k, r), ids("ru", k, r)
-                ids("up", k, r), ids("dn", k, r)
+        ids("xa", r), ids("xb", r), ids("rd", r)
         for k in range(chip_bits):
-            send("dc", k, r)
-            for i in range(1 << k):
-                send("up", k, r, i), send("dn", k, r, i)
-                recv("dc", k, r, i)
-    send("xc"), recv("xc")
-    for i in range(heads):
-        send("rs", i), recv("rs", i)
-    return send, recv
+            ids("xd", k, r), ids("ru", k, r), ids("up", k, r), ids("dn", k, r), ids("dc", k, r)
+    ids("xc")
+    for i in range(1, heads):
+        ids("rs", i)
+    return ids
 
 
 def kernel(chips, head_parts, seq_bits, qk_ref, v_ref, g_ref, lw_ref, qg_ref, vg_ref, lam_ref, car_ref,
@@ -55,7 +48,7 @@
     chip_bits = seq_bits - 1
     half = state // 2
     rows = half // CHUNKS
-    sid, rid = sem_ids(chips, head_parts, chip_bits)
+    sid = sem_ids(head_parts, chip_bits)
 
     seq, hd = lax.axis_index("seq"), lax.axis_index("head")
     core, z = seq % 2, seq // 2
@@ -76,11 +69,11 @@
 
     started = []
 
-    def send(cond, src, dst, skey, rkey, device):
+    def send(cond, src, dst, key, device):
         pltpu.make_async_remote_copy(
-            src_ref=src, dst_ref=dst, send_sem=ssem.at[sid(*skey)], recv_sem=rsem.at[rid(*rkey)],
+            src_ref=src, dst_ref=dst, send_sem=ssem.at[sid(*key)], recv_sem=rsem.at[sid(*key)],
             device_id=device, device_id_type=MESH).start()
-        started.append((cond, skey))
+        started.append((cond, key))
 
     def sent(skey):
         like = xd0 if skey[0] == "xc" else rs.at[skey[1]] if skey[0] == "rs" else bz.at[part(0)]
@@ -88,9 +81,9 @@
             src_ref=like, dst_ref=like, send_sem=ssem.at[sid(*skey)], recv_sem=rsem.at[0],
             device_id={"seq": partner}, device_id_type=MESH).wait_send()
 
-    def arrive(ref, rkey):
+    def arrive(ref, key):
         pltpu.make_async_remote_copy(
-            src_ref=ref, dst_ref=ref, send_sem=ssem.at[0], recv_sem=rsem.at[rid(*rkey)],
+            src_ref=ref, dst_ref=ref, send_sem=ssem.at[0], recv_sem=rsem.at[sid(*key)],
             device_id={"seq": partner}, device_id_type=MESH).wait_recv()
 
     barrier = pltpu.get_barrier_semaphore()
@@ -104,7 +97,7 @@
     own[...] = dot(qk, v_ref[...], 0, 0)
     pl.semaphore_wait(barrier, 1 + (chips - 1) + (head_parts - 1))
     for r in range(CHUNKS):
-        send(None, own.at[other(r)], xup.at[other(r)], ("xa", r), ("xa", r), {"seq": partner})
+        send(None, own.at[other(r)], xup.at[other(r)], ("xa", r), {"seq": partner})
 
     spread = (lax.broadcasted_iota(jnp.int32, (nheads, width), 1) // hdim
               == lax.broadcasted_iota(jnp.int32, (nheads, width), 0)).astype(F32).astype(BF16)
@@ -123,36 +116,30 @@
     for k in range(chip_bits - 1, -1, -1):
         grad_state(k + 1)
         for r in range(CHUNKS):
-            send(None, gst.at[k + 1, other(r)], xd.at[k, part(r)], ("xd", k, r), ("xd", k, r), {"seq": partner})
-
+            send(None, gst.at[k + 1, other(r)], xd.at[k, part(r)], ("xd", k, r), {"seq": partner})
+
+    lower = bit(0) == 0
     for r in range(CHUNKS):
         arrive(xup.at[mine(r)], ("xa", r))
         bz[part(r)] = own[mine(r)] + xup[mine(r)]
         if chip_bits:
-            cond = bit(0) == 0
-
-            @pl.when(cond)
-            def _():
-                send(cond, bz.at[part(r)], lst.at[0, mine(r)], ("up", 0, r, 0), ("up", 0, r), at_chip(z + 1))
-
-        for k in range(chip_bits - 1, -1, -1):
+            @pl.when(lower)
+            def _():
+                send(lower, bz.at[part(r)], lst.at[0, mine(r)], ("up", 0, r), at_chip(z + 1))
+
+    for k in range(chip_bits - 1, -1, -1):
+        size = 1 << k
+        top = (bit(k) == 1) & (z % size == size - 1)
+        for r in range(CHUNKS):
             arrive(xd.at[k, part(r)], ("xd", k, r))
             gz[k, part(r)] = gst[k + 1, mine(r)] + xd[k, part(r)]
-            size = 1 << k
-            under = z % size
-            if k == 0:
-                cond_d = bit(0) == 1
-
-                @pl.when(cond_d)
-                def _():
-                    send(cond_d, gz.at[0, part(r)], drec.at[0, part(r)], ("dn", 0, r, 0), ("dn", 0, r), at_chip(z - 1))
-            for i in range(1, size):
-                cond_c = (bit(k) == 1) & (under == i)
-
-                @pl.when(cond_c)
-                def _():
-                    send(cond_c, gz.at[k, part(r)], dcon.at[size - 1 - k + i - 1, part(r)],
-                         ("dc", k, r), ("dc", k, r, i), at_chip(z - i))
+
+            @pl.when(top)
+            def _():
+                if k == 0:
+                    send(top, gz.at[0, part(r)], drec.at[0, part(r)], ("dn", 0, r), at_chip(z - 1))
+                else:
+                    send(top, gz.at[k, part(r)], dcon.at[k, part(r)], ("dc", k, r), at_chip(z - 1))
 
     cond_low = core == 0
     cond_high = core == 1
@@ -160,13 +147,13 @@
     @pl.when(cond_low)
     def _():
         for r in range(CHUNKS):
-            send(cond_low, own.at[mine(r)], xup.at[mine(r)], ("xb", r), ("xb", r), {"seq": partner})
+            send(cond_low, own.at[mine(r)], xup.at[mine(r)], ("xb", r), {"seq": partner})
 
     grad_state(0)
 
     @pl.when(cond_high)
     def _():
-        send(cond_high, gst.at[0], xd0, ("xc",), ("xc",), {"seq": partner})
+        send(cond_high, gst.at[0], xd0, ("xc",), {"seq": partner})
 
     key_at = lax.broadcasted_iota(jnp.int32, (tok, tok), 0)
     query_at = lax.broadcasted_iota(jnp.int32, (tok, tok), 1)
@@ -216,17 +203,29 @@
             head_group(p * per, pl.ds(pl.multiple_of(p * per * hdim, per * hdim), per * hdim), per)
 
     def up_step(k, r):
+        size = 1 << k
         cond = bit(k) == 1
-
-        @pl.when(cond)
+        if k:
+            onward = cond & (z % size != size - 1)
+
+            @pl.when(onward)
+            def _():
+                arrive(lst.at[k, mine(r)], ("up", k, r))
+                send(onward, lst.at[k, mine(r)], lst.at[k, mine(r)], ("up", k, r), at_chip(z + 1))
+                send(onward, lst.at[k, mine(r)], lst.at[k, mine(r)], ("ru", k, r), {"seq": partner})
+
+            last = cond & (z % size == size - 1)
+        else:
+            last = cond
+
+        @pl.when(last)
         def _():
             arrive(lst.at[k, mine(r)], ("up", k, r))
-            send(cond, lst.at[k, mine(r)], lst.at[k, mine(r)], ("ru", k, r), ("ru", k, r), {"seq": partner})
+            send(last, lst.at[k, mine(r)], lst.at[k, mine(r)], ("ru", k, r), {"seq": partner})
 
         kk = k + 1
         if kk < chip_bits:
-            size = 1 << kk
-            cond_s = (z % size == size - 1) & (bit(kk) == 0)
+            cond_s = (z % (1 << kk) == (1 << kk) - 1) & (bit(kk) == 0)
 
             @pl.when(cond_s)
             def _():
@@ -234,37 +233,61 @@
                 for j in range(kk):
                     value = value + lst[j, mine(r)]
                 acc[kk, part(r)] = value
-                for i in range(size - 1, -1, -1):
-                    send(cond_s, acc.at[kk, part(r)], lst.at[kk, mine(r)], ("up", kk, r, i), ("up", kk, r),
-                         at_chip(z + 1 + i))
-
-            cond_d = (z % size == 0) & (bit(kk) == 1)
-
-            @pl.when(cond_d)
-            def _():
-                value = gz[kk, part(r)]
-                for i in range(1, size):
-                    slot = size - 1 - kk + i - 1
-                    arrive(dcon.at[slot, part(r)], ("dc", kk, r, i))
-                    value = value + dcon[slot, part(r)]
-                dsum[kk, part(r)] = value
-                for i in range(size):
-                    send(cond_d, dsum.at[kk, part(r)], drec.at[kk, part(r)], ("dn", kk, r, i), ("dn", kk, r),
-                         at_chip(z - size + i))
+                send(cond_s, acc.at[kk, part(r)], lst.at[kk, mine(r)], ("up", kk, r), at_chip(z + 1))
+
+    def sum_step(k, r):
+        size = 1 << k
+
+        def joined():
+            arrive(dcon.at[k, part(r)], ("dc", k, r))
+            dsum[k, part(r)] = gz[k, part(r)] + dcon[k, part(r)]
+
+        bottom = (bit(k) == 1) & (z % size == 0)
+
+        @pl.when(bottom)
+        def _():
+            joined()
+            send(bottom, dsum.at[k, part(r)], drec.at[k, part(r)], ("dn", k, r), at_chip(z - 1))
+
+        if k > 1:
+            middle = (bit(k) == 1) & (z % size != 0) & (z % size != size - 1)
+
+            @pl.when(middle)
+            def _():
+                joined()
+                send(middle, dsum.at[k, part(r)], dcon.at[k, part(r)], ("dc", k, r), at_chip(z - 1))
 
     has_back = z != chips - 1
 
-    def down_step(r):
-        bh[part(r)] = jnp.zeros((rows, width), F32)
-        for k in range(chip_bits):
-            @pl.when(bit(k) == 0)
-            def _():
-                arrive(drec.at[k, part(r)], ("dn", k, r))
-                bh[part(r)] = bh[part(r)] + drec[k, part(r)]
-
-        @pl.when(has_back)
-        def _():
-            send(has_back, bh.at[part(r)], bo.at[part(r)], ("rd", r), ("rd", r), {"seq": partner})
+    def down_step(k, r):
+        size = 1 << k
+        first = k == chip_bits - 1
+        cond = bit(k) == 0
+
+        @pl.when(cond)
+        def _():
+            arrive(drec.at[k, part(r)], ("dn", k, r))
+
+        if k:
+            onward = cond & (z % size != 0)
+
+            @pl.when(onward)
+            def _():
+                send(onward, drec.at[k, part(r)], drec.at[k, part(r)], ("dn", k, r), at_chip(z - 1))
+
+        @pl.when(cond)
+        def _():
+            bh[part(r)] = drec[k, part(r)] if first else bh[part(r)] + drec[k, part(r)]
+
+        if first:
+            @pl.when(jnp.logical_not(cond))
+            def _():
+                bh[part(r)] = jnp.zeros((rows, width), F32)
+
+        if k == 0:
+            @pl.when(has_back)
+            def _():
+                send(has_back, bh.at[part(r)], bo.at[part(r)], ("rd", r), {"seq": partner})
 
     def cross(b):
         state_low = low[b]
@@ -310,17 +333,23 @@
 
         cross(k + 1)
 
-    steps = [(lambda r=r: up_step(0, r)) for r in range(CHUNKS)] if chip_bits else []
-    steps.append(level_zero)
-    for k in range(1, chip_bits):
-        if k == chip_bits - 1:
-            for r in range(CHUNKS):
-                steps.append(lambda r=r, k=k: (up_step(k, r), down_step(r)))
+    steps = []
+    for k in range(chip_bits - 1):
+        for r in range(CHUNKS):
+            steps.append(lambda r=r, k=k: up_step(k, r))
+            steps.append(lambda r=r, k=chip_bits - 1 - k: sum_step(k, r))
+        if k == 0:
+            steps.append(level_zero)
         else:
-            steps += [(lambda r=r, k=k: up_step(k, r)) for r in range(CHUNKS)]
-    if chip_bits < 2:
-        steps += [(lambda r=r: down_step(r)) for r in range(CHUNKS)]
-    slots = min(5, max(1, groups))
+            steps.append(lambda k=k: level_up(k - 1))
+    for r in range(CHUNKS):
+        steps.append(lambda r=r: up_step(chip_bits - 1, r))
+        steps.append(lambda r=r: down_step(chip_bits - 1, r))
+    if chip_bits > 1:
+        steps.append(lambda: level_up(chip_bits - 2))
+    for k in range(chip_bits - 2, -1, -1):
+        steps += [(lambda r=r, k=k: down_step(k, r)) for r in range(CHUNKS)]
+    slots = min(10, max(1, groups))
     done = 0
     for n, step in enumerate(steps):
         upto = groups * min(slots, n * slots // len(steps) + 1) // slots
@@ -337,8 +366,7 @@
     rest = (at[...] - high.astype(F32)).astype(BF16)
     qp[...] = qp[...] + (dot(high, qk, 1, 0) + dot(high, qk, 0, 0)) + (dot(rest, qk, 1, 0) + dot(rest, qk, 0, 0))
 
-    for k in range(chip_bits):
-        level_up(k)
+    level_up(chip_bits - 1)
 
     @pl.when(has_back)
     def _():
@@ -365,7 +393,7 @@
     share = tok // head_parts
     for i in range(1, head_parts):
         to = (hd + i) % head_parts
-        send(None, qp.at[pl.ds(pl.multiple_of(to * share, share), share)], rs.at[i], ("rs", i), ("rs", i), {"head": to})
+        send(None, qp.at[pl.ds(pl.multiple_of(to * share, share), share)], rs.at[i], ("rs", i), {"head": to})
     vg_ref[...] = (vloc[...] + dot(qk, back, 1, 0)).astype(BF16)
     total = qp[pl.ds(pl.multiple_of(hd * share, share), share)]
     for i in range(1, head_parts):
@@ -382,6 +410,15 @@
                 sent(skey)
 
 
+def write_out(*refs):
+    sources, targets, sems = refs[:4], refs[4:8], refs[8]
+    copies = [pltpu.make_async_copy(source, target, sems.at[i]) for i, (source, target) in enumerate(zip(sources, targets))]
+    for copy in copies:
+        copy.start()
+    for copy in copies:
+        copy.wait()
+
+
 def solution(mesh):
     chips = mesh.shape["seq"] // 2
     head_parts = mesh.shape["head"]
@@ -393,19 +430,19 @@
         width = values.shape[1]
         nheads, levels = level_weights.shape[:2]
         half = state // 2
-        send, recv = sem_ids(chips, head_parts, chip_bits)
+        copies = len(sem_ids(head_parts, chip_bits).table)
         bits = max(1, chip_bits)
-        slots = max(1, (1 << chip_bits) - 1 - chip_bits)
         vm = pltpu.VMEM
         vspec = pl.BlockSpec(memory_space=pltpu.VMEM)
-        return pl.pallas_call(
+        shapes = (
+            ((tok // head_parts, state), F32),
+            ((tok, width), BF16),
+            ((nheads, levels, tok), F32),
+            ((1, state, width), F32),
+        )
+        results = pl.pallas_call(
             functools.partial(kernel, chips, head_parts, seq_bits),
-            out_shape=(
-                jax.ShapeDtypeStruct((tok // head_parts, state), F32),
-                jax.ShapeDtypeStruct((tok, width), BF16),
-                jax.ShapeDtypeStruct((nheads, levels, tok), F32),
-                jax.ShapeDtypeStruct((1, state, width), F32),
-            ),
+            out_shape=tuple(pltpu.VMEM(shape, kind) for shape, kind in shapes),
             in_specs=[vspec] * 4,
             out_specs=(vspec,) * 4,
             scratch_shapes=[
@@ -419,7 +456,7 @@
                 vm((bits, half, width), F32),
                 vm((bits, half, width), F32),
                 vm((bits, state, width), F32),
-                vm((slots, half, width), F32),
+                vm((bits, half, width), F32),
                 vm((bits, half, width), F32),
                 vm((half, width), F32),
                 vm((half, width), F32),
@@ -432,12 +469,19 @@
                 vm((tok, state), F32),
                 vm((head_parts, tok // head_parts, state), F32),
                 vm((2, tok, tok), F32),
-                pltpu.SemaphoreType.DMA((len(send.table),)),
-                pltpu.SemaphoreType.DMA((len(recv.table),)),
+                pltpu.SemaphoreType.DMA((copies,)),
+                pltpu.SemaphoreType.DMA((copies,)),
             ],
             compiler_params=pltpu.CompilerParams(
                 collective_id=0, has_side_effects=True, vmem_limit_bytes=56 * 1024 * 1024),
         )(qk_proj, values, out_grad, level_weights)
+        return pl.pallas_call(
+            write_out,
+            out_shape=tuple(jax.ShapeDtypeStruct(shape, kind) for shape, kind in shapes),
+            in_specs=[vspec] * 4,
+            out_specs=(pl.BlockSpec(memory_space=pl.ANY),) * 4,
+            scratch_shapes=[pltpu.SemaphoreType.DMA((4,))],
+        )(*(pltpu.with_memory_space_constraint(x, pltpu.VMEM) for x in results))
 
     return jax.shard_map(
         body, mesh=mesh,

time: 41 us -> 35.7 us (0.87)
  local copies, waits for them, and re-layouts: 5.54 us -> 0 us
    unnamed x6 -> x0, local copies, waits for them, and re-layouts: 5.54 us -> none
    pallas_call x0 -> x1, Pallas kernels: none -> 1.04 us  [body(): pl.pallas_call(write_out, out_shape=tuple((jax.ShapeDtypeStruct(shape, ki...]
    pallas_call x1, Pallas kernels: 34.6 us -> 33.9 us  [body(): pl.pallas_call(functools.partial(kernel, chips, head_parts, seq_bits), ou...]
where the time goes in v2:
time: 35.7 us; the launch traced here: 35.6 us
  Pallas kernels  34.9 us (98%)
  between operations  0.64 us (2%)
    pallas_call x1, Pallas kernels, body(): pl.pallas_call(functools.partial(kernel, chips, head_parts, seq_bits), ou...  33.9 us
    pallas_call x1, Pallas kernels, body(): pl.pallas_call(write_out, out_shape=tuple((jax.ShapeDtypeStruct(shape, ki...  1.04 us

profile of v2, /device:TPU:0, one launch (start us, length us, event | category | flops | bytes accessed | tf_op | source)
XLA Modules:
  0.0 35.6 jit_solution(10944584514209664855)
XLA Ops:
  0.6 33.9 %shard_map.75 = (f32[32,128]{1,0:T(8,128)S(1)}, bf16[128,1280]{1,0:T(8,128)(2,1)S(1)}, f32[20,16,128]{2,1,0:T(8,128)S(1)}, f32[1,128,1280]{2,1,0:T(8,128)S(1)}) custom-call(bf16[128,128]{1,0:T(8,128)(2,1)} %qk_ref.1, bf16[128,1280]{1,0:T(8,128)(2,1)} %v_ref.1, bf16[128,1280]{1,0:T(8,128)(2,1)} %g_ref.1, f32[20,16,128]{2,1,0:T(8,128)} %lw_ref.1), custom_call_target="tpu_custom_call" | custom-call | tf_op jit(solution)/shard_map/pallas_call | solution.py:443
  34.5 1.0 %shard_map.76 = (f32[32,128]{1,0:T(8,128)}, bf16[128,1280]{1,0:T(8,128)(2,1)}, f32[20,16,128]{2,1,0:T(8,128)}, f32[1,128,1280]{2,1,0:T(8,128)}) custom-call(f32[32,128]{1,0:T(8,128)S(1)} %get-tuple-element.8.refs_0_, bf16[128,1280]{1,0:T(8,128)(2,1)S(1)} %get-tuple-element.9.refs_1_, f32[20,16,128]{2,1,0:T(8,128)S(1)} %get-tuple-element.10.refs_2_, ...), custom_call_target="tpu_custom_call" | custom-call | tf_op jit(solution)/shard_map/pallas_call | solution.py:478

commit v3 on v2

--- a/solution.py
+++ b/solution.py
@@ -8,7 +8,7 @@
 from jax.sharding import PartitionSpec as P
 
 MESH = pl.DeviceIdType.MESH
-CHUNKS = 8
+CHUNKS = 4
 F32 = jnp.float32
 BF16 = jnp.bfloat16
 
@@ -37,9 +37,13 @@
     return ids
 
 
-def kernel(chips, head_parts, seq_bits, qk_ref, v_ref, g_ref, lw_ref, qg_ref, vg_ref, lam_ref, car_ref,
+def kernel(chips, head_parts, seq_bits, qk_in, v_in, g_in, lw_in, qg_ref, vg_ref, lam_ref, car_ref,
            own, gst, xup, xd0, xd, bz, gz, acc, dsum, lst, dcon, drec, bh, bo, bst, low, blow, sc, vloc, at, qp, rs,
-           lev_ref, ssem, rsem):
+           lev_ref, qk_ref, v_ref, g_ref, lw_ref, isem, ssem, rsem):
+    loads = [pltpu.make_async_copy(source, target, isem.at[i]) for i, (source, target) in
+             enumerate(((qk_in, qk_ref), (v_in, v_ref), (g_in, g_ref), (lw_in, lw_ref)))]
+    for load in loads:
+        load.start()
     tok, state = qk_ref.shape
     width = v_ref.shape[1]
     nheads, levels = lw_ref.shape[0], lw_ref.shape[1]
@@ -93,12 +97,16 @@
     for i in range(1, head_parts):
         pl.semaphore_signal(barrier, inc=1, device_id={"head": (hd + i) % head_parts}, device_id_type=MESH)
 
+    loads[0].wait()
+    loads[1].wait()
     qk = qk_ref[...]
     own[...] = dot(qk, v_ref[...], 0, 0)
     pl.semaphore_wait(barrier, 1 + (chips - 1) + (head_parts - 1))
     for r in range(CHUNKS):
         send(None, own.at[other(r)], xup.at[other(r)], ("xa", r), {"seq": partner})
 
+    loads[2].wait()
+    loads[3].wait()
     spread = (lax.broadcasted_iota(jnp.int32, (nheads, width), 1) // hdim
               == lax.broadcasted_iota(jnp.int32, (nheads, width), 0)).astype(F32).astype(BF16)
 
@@ -289,18 +297,15 @@
             def _():
                 send(has_back, bh.at[part(r)], bo.at[part(r)], ("rd", r), {"seq": partner})
 
-    def cross(b):
-        state_low = low[b]
-        readout = dot(qk, state_low, 1, 0)
-        product = readout * g_ref[...].astype(F32)
+    def query(b):
+        part_b = dot(sc[b], low[b], 1, 1)
+        qp[...] = part_b if b == 0 else qp[...] + part_b
+
+    def level_sums(b):
+        product = dot(qk, low[b], 1, 0) * g_ref[...].astype(F32)
         high = product.astype(BF16)
         rest = (product - high.astype(F32)).astype(BF16)
         lam_ref[:, tok_bits + 1 + b, :] = dot(spread, high, 1, 1) + dot(spread, rest, 1, 1)
-        part_b = dot(sc[b], state_low, 1, 1)
-        if b == 0:
-            qp[...] = part_b
-        else:
-            qp[...] = qp[...] + part_b
 
     def level_zero():
         @pl.when(core == 1)
@@ -315,9 +320,10 @@
             low[0] = jnp.zeros((state, width), BF16)
             car_ref[0] = jnp.zeros((state, width), F32)
 
-        cross(0)
-
-    def level_up(k):
+        query(0)
+        level_sums(0)
+
+    def level_arrive(k):
         cond = bit(k) == 1
 
         @pl.when(cond)
@@ -325,29 +331,43 @@
             for r in range(CHUNKS):
                 arrive(lst.at[k, other(r)], ("ru", k, r))
             low[k + 1] = lst[k].astype(BF16)
+
+        @pl.when(jnp.logical_not(cond))
+        def _():
+            low[k + 1] = jnp.zeros((state, width), BF16)
+
+        query(k + 1)
+
+    def level_finish(k):
+        @pl.when(bit(k) == 1)
+        def _():
             car_ref[0] = car_ref[0] + lst[k]
 
-        @pl.when(jnp.logical_not(cond))
-        def _():
-            low[k + 1] = jnp.zeros((state, width), BF16)
-
-        cross(k + 1)
+        level_sums(k + 1)
+
+    def level_up(k):
+        level_arrive(k)
+        level_finish(k)
 
     steps = []
-    for k in range(chip_bits - 1):
+    final = chip_bits - 1
+    early = []
+    for k in range(final):
         for r in range(CHUNKS):
-            steps.append(lambda r=r, k=k: up_step(k, r))
-            steps.append(lambda r=r, k=chip_bits - 1 - k: sum_step(k, r))
-        if k == 0:
-            steps.append(level_zero)
-        else:
-            steps.append(lambda k=k: level_up(k - 1))
-    for r in range(CHUNKS):
-        steps.append(lambda r=r: up_step(chip_bits - 1, r))
-        steps.append(lambda r=r: down_step(chip_bits - 1, r))
-    if chip_bits > 1:
-        steps.append(lambda: level_up(chip_bits - 2))
-    for k in range(chip_bits - 2, -1, -1):
+            early.append((lambda r=r, k=k: up_step(k, r), lambda r=r, k=final - k: sum_step(k, r)))
+        early.append((level_zero,) if k == 0 else (lambda k=k: level_up(k - 1),))
+    late = [(lambda r=r: up_step(final, r), lambda r=r: down_step(final, r)) for r in range(CHUNKS)]
+    if not early:
+        early = [(level_zero,)]
+    lead = len(early) - CHUNKS + 1 if final == 1 else len(early)
+    steps += [one for pair in early[:lead] for one in pair]
+    for pair, after in zip(late, early[lead:] + [()] * CHUNKS):
+        steps += list(pair) + list(after)
+    for after in early[lead:][CHUNKS:]:
+        steps += list(after)
+    if final > 0:
+        steps.append(lambda: level_up(final - 1))
+    for k in range(final - 1, -1, -1):
         steps += [(lambda r=r, k=k: down_step(k, r)) for r in range(CHUNKS)]
     slots = min(10, max(1, groups))
     done = 0
@@ -366,7 +386,7 @@
     rest = (at[...] - high.astype(F32)).astype(BF16)
     qp[...] = qp[...] + (dot(high, qk, 1, 0) + dot(high, qk, 0, 0)) + (dot(rest, qk, 1, 0) + dot(rest, qk, 0, 0))
 
-    level_up(chip_bits - 1)
+    level_arrive(final)
 
     @pl.when(has_back)
     def _():
@@ -394,6 +414,7 @@
     for i in range(1, head_parts):
         to = (hd + i) % head_parts
         send(None, qp.at[pl.ds(pl.multiple_of(to * share, share), share)], rs.at[i], ("rs", i), {"head": to})
+    level_finish(final)
     vg_ref[...] = (vloc[...] + dot(qk, back, 1, 0)).astype(BF16)
     total = qp[pl.ds(pl.multiple_of(hd * share, share), share)]
     for i in range(1, head_parts):
@@ -443,7 +464,7 @@
         results = pl.pallas_call(
             functools.partial(kernel, chips, head_parts, seq_bits),
             out_shape=tuple(pltpu.VMEM(shape, kind) for shape, kind in shapes),
-            in_specs=[vspec] * 4,
+            in_specs=[pl.BlockSpec(memory_space=pl.ANY)] * 4,
             out_specs=(vspec,) * 4,
             scratch_shapes=[
                 vm((state, width), F32),
@@ -469,6 +490,11 @@
                 vm((tok, state), F32),
                 vm((head_parts, tok // head_parts, state), F32),
                 vm((2, tok, tok), F32),
+                vm((tok, state), BF16),
+                vm((tok, width), BF16),
+                vm((tok, width), BF16),
+                vm((nheads, levels, tok), F32),
+                pltpu.SemaphoreType.DMA((4,)),
                 pltpu.SemaphoreType.DMA((copies,)),
                 pltpu.SemaphoreType.DMA((copies,)),
             ],

time: 35.7 us -> 33.8 us (0.947)
  Pallas kernels: 34.9 us -> 33 us
    pallas_call x1, Pallas kernels: 33.9 us -> 31.9 us  [body(): pl.pallas_call(functools.partial(kernel, chips, head_parts, seq_bits), ou...]
where the time goes in v3:
time: 33.8 us; the launch traced here: 33.6 us
  Pallas kernels  33 us (98%)
  between operations  0.64 us (2%)
    pallas_call x1, Pallas kernels, body(): pl.pallas_call(functools.partial(kernel, chips, head_parts, seq_bits), ou...  31.9 us
    pallas_call x1, Pallas kernels, body(): pl.pallas_call(write_out, out_shape=tuple((jax.ShapeDtypeStruct(shape, ki...  1.04 us

profile of v3, /device:TPU:0, one launch (start us, length us, event | category | flops | bytes accessed | tf_op | source)
XLA Modules:
  0.0 33.6 jit_solution(13753284221374288229)
XLA Ops:
  0.6 31.9 %shard_map.75 = (f32[32,128]{1,0:T(8,128)S(1)}, bf16[128,1280]{1,0:T(8,128)(2,1)S(1)}, f32[20,16,128]{2,1,0:T(8,128)S(1)}, f32[1,128,1280]{2,1,0:T(8,128)S(1)}) custom-call(bf16[128,128]{1,0:T(8,128)(2,1)} %qk_in.1, bf16[128,1280]{1,0:T(8,128)(2,1)} %v_in.1, bf16[128,1280]{1,0:T(8,128)(2,1)} %g_in.1, f32[20,16,128]{2,1,0:T(8,128)} %lw_in.1), custom_call_target="tpu_custom_call" | custom-call | tf_op jit(solution)/shard_map/pallas_call | solution.py:464
  32.6 1.0 %shard_map.76 = (f32[32,128]{1,0:T(8,128)}, bf16[128,1280]{1,0:T(8,128)(2,1)}, f32[20,16,128]{2,1,0:T(8,128)}, f32[1,128,1280]{2,1,0:T(8,128)}) custom-call(f32[32,128]{1,0:T(8,128)S(1)} %get-tuple-element.8.refs_0_, bf16[128,1280]{1,0:T(8,128)(2,1)S(1)} %get-tuple-element.9.refs_1_, f32[20,16,128]{2,1,0:T(8,128)S(1)} %get-tuple-element.10.refs_2_, ...), custom_call_target="tpu_custom_call" | custom-call | tf_op jit(solution)/shard_map/pallas_call | solution.py:504

commit v4 on v3

--- a/solution.py
+++ b/solution.py
@@ -359,7 +359,7 @@
     late = [(lambda r=r: up_step(final, r), lambda r=r: down_step(final, r)) for r in range(CHUNKS)]
     if not early:
         early = [(level_zero,)]
-    lead = len(early) - CHUNKS + 1 if final == 1 else len(early)
+    lead = len(early) - CHUNKS + 2 if final == 1 else len(early)
     steps += [one for pair in early[:lead] for one in pair]
     for pair, after in zip(late, early[lead:] + [()] * CHUNKS):
         steps += list(pair) + list(after)

time: 33.8 us -> 33 us (0.976)
  Pallas kernels: 33 us -> 32.2 us
    pallas_call x1, Pallas kernels: 31.9 us -> 31.1 us  [body(): pl.pallas_call(functools.partial(kernel, chips, head_parts, seq_bits), ou...]
where the time goes in v4:
time: 33 us; the launch traced here: 32.8 us
  Pallas kernels  32.2 us (98%)
  between operations  0.64 us (2%)
    pallas_call x1, Pallas kernels, body(): pl.pallas_call(functools.partial(kernel, chips, head_parts, seq_bits), ou...  31.1 us
    pallas_call x1, Pallas kernels, body(): pl.pallas_call(write_out, out_shape=tuple((jax.ShapeDtypeStruct(shape, ki...  1.04 us

profile of v4, /device:TPU:0, one launch (start us, length us, event | category | flops | bytes accessed | tf_op | source)
XLA Modules:
  0.0 32.8 jit_solution(15646851347708894356)
XLA Ops:
  0.6 31.1 %shard_map.75 = (f32[32,128]{1,0:T(8,128)S(1)}, bf16[128,1280]{1,0:T(8,128)(2,1)S(1)}, f32[20,16,128]{2,1,0:T(8,128)S(1)}, f32[1,128,1280]{2,1,0:T(8,128)S(1)}) custom-call(bf16[128,128]{1,0:T(8,128)(2,1)} %qk_in.1, bf16[128,1280]{1,0:T(8,128)(2,1)} %v_in.1, bf16[128,1280]{1,0:T(8,128)(2,1)} %g_in.1, f32[20,16,128]{2,1,0:T(8,128)} %lw_in.1), custom_call_target="tpu_custom_call" | custom-call | tf_op jit(solution)/shard_map/pallas_call | solution.py:464
  31.8 1.0 %shard_map.76 = (f32[32,128]{1,0:T(8,128)}, bf16[128,1280]{1,0:T(8,128)(2,1)}, f32[20,16,128]{2,1,0:T(8,128)}, f32[1,128,1280]{2,1,0:T(8,128)}) custom-call(f32[32,128]{1,0:T(8,128)S(1)} %get-tuple-element.8.refs_0_, bf16[128,1280]{1,0:T(8,128)(2,1)S(1)} %get-tuple-element.9.refs_1_, f32[20,16,128]{2,1,0:T(8,128)S(1)} %get-tuple-element.10.refs_2_, ...), custom_call_target="tpu_custom_call" | custom-call | tf_op jit(solution)/shard_map/pallas_call | solution.py:504
